TPU v7x, 32 devices: a whole 2x2x4 slice. The times are simulated.
32 devices in a mesh: groups: 2 (over y), space: 8 (over z, x), tm: 2 (over core).
Axes of the slice: x: 2, y: 2, z: 4, core: 2. Of those that a mesh axis runs over, the one named last changes fastest.
Arguments:
- base_latent: bfloat16 [64, 2, 12, 128], P(('groups', 'space'), 'tm'), parts along dimension 0, may hold values from -6 to 6
- cotangent: bfloat16 [64, 8, 48, 128], P(('groups', 'space'), 'tm'), parts along dimension 0, may hold values from -6 to 6
- w_spatial: bfloat16 [3, 3, 128, 128], replicated, may hold values from -0.1875 to 0.1875
- w_temporal: bfloat16 [5, 128, 128], replicated, may hold values from -0.25 to 0.25
Outputs:
- result: bfloat16 [64, 8, 48, 128], P(('groups', 'space'), 'tm'), parts along dimension 0
- grad_base: float32 [64, 2, 12, 128], P(('groups', 'space'), 'tm'), parts along dimension 0
- grad_spatial: float32 [6, 3, 128, 128], P('groups'), parts along dimension 0
- grad_temporal: float32 [10, 128, 128], P('groups'), parts along dimension 0
There are 2 independent parts, one for each index of `groups`. A program takes and returns all parts, laid end to end along the dimension named above; an argument that names none is the same for every part. Nothing has to cross between parts.
All inputs are finite; a program needn't handle non-finite values.
Results may differ from a plain program's by a relative error of at most 0.0064.
Values may be sent and summed in bfloat16 or wider, within the bound.
No kernel may reach another device: no remote copies, remote signals or barrier semaphores. Data moves between devices by JAX's collectives and lax.ppermute only.
A program may use at most 64 MiB of HBM per device.

v0:
```python
import jax
import jax.numpy as jnp
from jax import lax
from jax.sharding import PartitionSpec as P

FRAME_DILATION = 2


def shifted(value, axis, by):
    count = lax.axis_size(axis)
    pairs = [(i, i + by) for i in range(count) if 0 <= i + by < count]
    return lax.ppermute(value, axis, pairs)


def extended(cells, sides, width):
    for axis, dim in sides:
        count = lax.axis_size(axis)
        ends = count - 1
        head = lax.slice_in_dim(cells, 0, width, axis=dim)
        tail = lax.slice_in_dim(cells, cells.shape[dim] - width, cells.shape[dim], axis=dim)
        cells = jnp.concatenate(
            [
                lax.ppermute(tail, axis, [(i, (i + 1) % count) for i in range(ends)]),
                cells,
                lax.ppermute(head, axis, [((i + 1) % count, i) for i in range(ends)]),
            ],
            axis=dim,
        )
    return cells


def widen_cols(field):
    left_cols = jnp.concatenate([field[:, :, :1], field[:, :, :-1]], axis=2)
    right_cols = jnp.concatenate([field[:, :, 1:], field[:, :, -1:]], axis=2)
    phases = jnp.stack(
        [
            0.375 * left_cols + 0.625 * field,
            0.125 * left_cols + 0.875 * field,
            0.875 * field + 0.125 * right_cols,
            0.625 * field + 0.375 * right_cols,
        ],
        axis=3,
    )
    return phases.reshape(field.shape[0], field.shape[1], field.shape[2] * 4, field.shape[3])


def widen_rows(below_rows, middle, above_rows):
    phases = jnp.stack(
        [
            0.375 * below_rows + 0.625 * middle,
            0.125 * below_rows + 0.875 * middle,
            0.875 * middle + 0.125 * above_rows,
            0.625 * middle + 0.375 * above_rows,
        ],
        axis=2,
    )
    return phases.reshape(middle.shape[0], middle.shape[1] * 4, middle.shape[2], middle.shape[3])


def silu_slope(value):
    sigmoid_val = jax.nn.sigmoid(value)
    return sigmoid_val * (1.0 + value * (1.0 - sigmoid_val))


def conv_three(padded, weight, row_count, col_count, start):
    frame_count = padded.shape[0]
    channels = weight.shape[3]
    summed = jnp.zeros((frame_count * row_count * col_count, channels), jnp.float32)
    for tap_row in range(3):
        for tap_col in range(3):
            r0 = start - tap_row if start else tap_row
            c0 = start - tap_col if start else tap_col
            frame_window = padded[:, r0 : r0 + row_count, c0 : c0 + col_count].reshape(
                -1, padded.shape[3]
            )
            kernel = weight[tap_row, tap_col] if not start else weight[tap_row, tap_col].T
            summed = summed + jnp.dot(frame_window, kernel, preferred_element_type=jnp.float32)
    return summed.reshape(frame_count, row_count, col_count, channels)


def space_grads(padded, delta, row_count, col_count):
    flat = delta.reshape(-1, delta.shape[3])
    taps = []
    for tap_row in range(3):
        for tap_col in range(3):
            frame_window = padded[
                :, tap_row : tap_row + row_count, tap_col : tap_col + col_count
            ].reshape(-1, padded.shape[3])
            taps.append(
                lax.dot_general(
                    frame_window, flat, (((0,), (0,)), ((), ())), preferred_element_type=jnp.float32
                )
            )
    return jnp.stack(taps).reshape(3, 3, padded.shape[3], delta.shape[3])


def conv_time(frames_extended, weight, frame_count, reversed_order):
    channels = weight.shape[2]
    tensor_shape = frames_extended.shape
    summed = jnp.zeros((frame_count * tensor_shape[1] * tensor_shape[2], channels), jnp.float32)
    for kernel_tap in range(5):
        frame_offset = (
            (4 - kernel_tap) * FRAME_DILATION if reversed_order else kernel_tap * FRAME_DILATION
        )
        frame_window = frames_extended[frame_offset : frame_offset + frame_count].reshape(
            -1, tensor_shape[3]
        )
        kernel = weight[kernel_tap].T if reversed_order else weight[kernel_tap]
        summed = summed + jnp.dot(frame_window, kernel, preferred_element_type=jnp.float32)
    return summed.reshape(frame_count, tensor_shape[1], tensor_shape[2], channels)


def time_grads(frames_extended, delta, frame_count):
    flat = delta.reshape(-1, delta.shape[3])
    taps = []
    for kernel_tap in range(5):
        frame_window = frames_extended[
            kernel_tap * FRAME_DILATION : kernel_tap * FRAME_DILATION + frame_count
        ].reshape(-1, frames_extended.shape[3])
        taps.append(
            lax.dot_general(
                frame_window, flat, (((0,), (0,)), ((), ())), preferred_element_type=jnp.float32
            )
        )
    return jnp.stack(taps)


def shrink_base(grad_image, row_rank, row_devices, latent_shape):
    frame_count, low_rows, low_cols, channels = latent_shape
    _, col_pull = jax.vjp(
        widen_cols, jnp.zeros((frame_count, grad_image.shape[1], low_cols, channels), jnp.float32)
    )
    narrow = col_pull(grad_image)[0].reshape(frame_count, low_rows, 4, low_cols, channels)
    to_lower = 0.375 * narrow[:, :, 0] + 0.125 * narrow[:, :, 1]
    to_middle = (
        0.625 * narrow[:, :, 0]
        + 0.875 * narrow[:, :, 1]
        + 0.875 * narrow[:, :, 2]
        + 0.625 * narrow[:, :, 3]
    )
    to_upper = 0.125 * narrow[:, :, 2] + 0.375 * narrow[:, :, 3]
    from_above = shifted(to_lower, "tm", -1)
    from_below = shifted(to_upper, "tm", 1)
    next_lower = jnp.concatenate([to_lower[:, 1:], from_above], axis=1)
    prev_upper = jnp.concatenate([from_below, to_upper[:, :-1]], axis=1)
    edge_low = jnp.where(row_rank == 0, to_lower, jnp.zeros_like(to_lower))
    edge_high = jnp.where(row_rank == row_devices - 1, to_upper, jnp.zeros_like(to_upper))
    empty_rows = jnp.zeros((frame_count, low_rows - 1, low_cols, channels), jnp.float32)
    summed = to_middle + next_lower + prev_upper
    return (
        summed
        + jnp.concatenate([edge_low, empty_rows], axis=1)
        + jnp.concatenate([empty_rows, edge_high], axis=1)
    )


def local(base_latent, cotangent, w_spatial, w_temporal):
    row_rank = lax.axis_index("tm")
    row_devices = lax.axis_size("tm")
    padded_base = extended(base_latent, (("tm", 1),), 1)
    low_first = jnp.where(row_rank == 0, base_latent, padded_base[:, :1])
    high_last = jnp.where(row_rank == row_devices - 1, base_latent, padded_base[:, -1:])
    latent32 = base_latent.astype(jnp.float32)
    below_rows = jnp.concatenate([low_first, base_latent[:, :-1]], axis=1).astype(jnp.float32)
    above_rows = jnp.concatenate([base_latent[:, 1:], high_last], axis=1).astype(jnp.float32)
    upsampled = widen_cols(widen_rows(below_rows, latent32, above_rows)).astype(jnp.bfloat16)
    frame_count, row_count, col_count = (upsampled.shape[0], upsampled.shape[1], upsampled.shape[2])
    image_ext = extended(upsampled, (("tm", 1),), 1)
    padded = jnp.pad(image_ext, ((0, 0), (0, 0), (1, 1), (0, 0)))
    pre_one = conv_three(padded, w_spatial, row_count, col_count, 0)
    first_activation = jax.nn.silu(pre_one).astype(jnp.bfloat16)
    frames_extended = extended(first_activation, (("space", 0),), 2 * FRAME_DILATION)
    pre_two = conv_time(frames_extended, w_temporal, frame_count, False)
    result = (upsampled.astype(jnp.float32) + jax.nn.silu(pre_two)).astype(jnp.bfloat16)
    upstream = cotangent.astype(jnp.float32)
    second_gradient = (upstream * silu_slope(pre_two)).astype(jnp.bfloat16)
    temporal_local = time_grads(frames_extended, second_gradient, frame_count)
    grad_temporal = lax.psum(temporal_local, ("space", "tm"))
    gradient_extended = extended(second_gradient, (("space", 0),), 2 * FRAME_DILATION)
    back_one = conv_time(gradient_extended, w_temporal, frame_count, True)
    delta_one = (back_one * silu_slope(pre_one)).astype(jnp.bfloat16)
    spatial_local = space_grads(padded, delta_one, row_count, col_count)
    delta_rows = extended(delta_one, (("tm", 1),), 1)
    delta_pad = jnp.pad(delta_rows, ((0, 0), (0, 0), (1, 1), (0, 0)))
    grad_image = upstream + conv_three(delta_pad, w_spatial, row_count, col_count, 2)
    grad_base = shrink_base(grad_image, row_rank, row_devices, base_latent.shape)
    grad_spatial = lax.psum(spatial_local, ("space", "tm"))
    return (result, grad_base, grad_spatial, grad_temporal)


def solution(mesh):
    in_specs = (
        P(("groups", "space"), "tm", None, None),
        P(("groups", "space"), "tm", None, None),
        P(),
        P(),
    )
    out_specs = (
        P(("groups", "space"), "tm", None, None),
        P(("groups", "space"), "tm", None, None),
        P("groups", None, None, None),
        P("groups", None, None),
    )
    return jax.shard_map(local, mesh=mesh, in_specs=in_specs, out_specs=out_specs, check_vma=False)
```

profile of v0, /device:TPU:0, one launch (start us, length us, event | category | flops | bytes accessed | tf_op | source)
XLA Modules:
  0.0 162.9 jit_solution(3683068652345166377)
XLA Ops:
  7.2 0.8 copy.55
  8.0 2.4 %collective-permute-start = (bf16[4,1,12,128]{3,1,2,0:T(2,128)(2,1)S(1)}, bf16[4,1,12,128]{3,1,2,0:T(2,128)(2,1)S(1)}, u32[]{:S(2)}, u32[]{:S(2)}) collective-permute-start(bf16[4,1,12,128]{3,1,2,0:T(2,128)(2,1)S(1)} %copy.55), channel_id=1, source_target_pairs={{0,1},{2,3},{4,5},{6,7},{8,9},{10,11},{12,13},{14,15},{16,17},{18,... | collective-permute-start | bytes 36872 | tf_op jit(solution)/shard_map/ppermute | solution.py:23
  10.4 1.3 collective-permute-start.1
  11.7 1.8 %collective-permute-done.1 = bf16[4,1,12,128]{3,1,2,0:T(2,128)(2,1)S(1)} collective-permute-done((bf16[4,1,12,128]{3,1,2,0:T(2,128)(2,1)S(1)}, bf16[4,1,12,128]{3,1,2,0:T(2,128)(2,1)S(1)}, u32[]{:S(2)}, u32[]{:S(2)}) %collective-permute-start.1) | collective-permute-done | bytes 12320 | tf_op jit(solution)/shard_map/ppermute | solution.py:25
  14.4 2.1 %collective-permute-start.2 = (bf16[4,1,48,128]{3,2,1,0:T(8,128)(2,1)S(1)}, bf16[4,1,48,128]{3,2,1,0:T(8,128)(2,1)S(1)}, u32[]{:S(2)}, u32[]{:S(2)}) collective-permute-start(bf16[4,1,48,128]{3,2,1,0:T(8,128)(2,1)S(1)} %get-tuple-element.34), channel_id=1, source_target_pairs={{0,1},{2,3},{4,5},{6,7},{8,9},{10,11},{12,13},{14,15},{16,17},{18,... | collective-permute-start | bytes 147464 | tf_op jit(solution)/shard_map/ppermute | solution.py:23
  16.5 1.3 collective-permute-start.3
  17.8 1.8 %collective-permute-done.3 = bf16[4,1,48,128]{3,2,1,0:T(8,128)(2,1)S(1)} collective-permute-done((bf16[4,1,48,128]{3,2,1,0:T(8,128)(2,1)S(1)}, bf16[4,1,48,128]{3,2,1,0:T(8,128)(2,1)S(1)}, u32[]{:S(2)}, u32[]{:S(2)}) %collective-permute-start.3) | collective-permute-done | bytes 49184 | tf_op jit(solution)/shard_map/ppermute | solution.py:25
  19.9 0.8 copy-done
  22.7 4.2 %collective-permute-start.4 = (bf16[4,4,48,128]{3,2,1,0:T(8,128)(2,1)S(1)}, bf16[4,4,48,128]{3,2,1,0:T(8,128)(2,1)S(1)}, u32[]{:S(2)}, u32[]{:S(2)}) collective-permute-start(bf16[4,4,48,128]{3,2,1,0:T(8,128)(2,1)S(1)} %multiply_convert_fusion.3), channel_id=1, source_target_pairs={{0,2},{2,4},{4,6},{6,8},{8,10},{10,12},{12,14},{1,3},{3,5},{5,7},{... | collective-permute-start | bytes 589832 | tf_op jit(solution)/shard_map/ppermute | solution.py:23
  26.9 1.3 collective-permute-start.5
  28.4 3.0 %collective-permute-done.4 = bf16[4,4,48,128]{3,2,1,0:T(8,128)(2,1)S(1)} collective-permute-done((bf16[4,4,48,128]{3,2,1,0:T(8,128)(2,1)S(1)}, bf16[4,4,48,128]{3,2,1,0:T(8,128)(2,1)S(1)}, u32[]{:S(2)}, u32[]{:S(2)}) %collective-permute-start.4) | collective-permute-done | bytes 196640 | tf_op jit(solution)/shard_map/ppermute | solution.py:23
  31.4 4.0 %collective-permute-done.5 = bf16[4,4,48,128]{3,2,1,0:T(8,128)(2,1)S(1)} collective-permute-done((bf16[4,4,48,128]{3,2,1,0:T(8,128)(2,1)S(1)}, bf16[4,4,48,128]{3,2,1,0:T(8,128)(2,1)S(1)}, u32[]{:S(2)}, u32[]{:S(2)}) %collective-permute-start.5) | collective-permute-done | bytes 196640 | tf_op jit(solution)/shard_map/ppermute | solution.py:25
  36.3 0.7 copy-done.1
  37.0 0.9 fusion.21
  37.9 1.3 collective-permute-start.6
  39.2 5.1 %collective-permute-start.7 = (bf16[4,4,48,128]{3,2,1,0:T(8,128)(2,1)S(1)}, bf16[4,4,48,128]{3,2,1,0:T(8,128)(2,1)S(1)}, u32[]{:S(2)}, u32[]{:S(2)}) collective-permute-start(bf16[4,4,48,128]{3,2,1,0:T(8,128)(2,1)S(1)} %get-tuple-element.10), channel_id=1, source_target_pairs={{0,2},{2,4},{4,6},{6,8},{8,10},{10,12},{12,14},{1,3},{3,5},{5,7},{... | collective-permute-start | bytes 589832 | tf_op jit(solution)/shard_map/ppermute | solution.py:23
  45.9 0.6 collective-permute-done.6
  46.5 5.2 %collective-permute-done.7 = bf16[4,4,48,128]{3,2,1,0:T(8,128)(2,1)S(1)} collective-permute-done((bf16[4,4,48,128]{3,2,1,0:T(8,128)(2,1)S(1)}, bf16[4,4,48,128]{3,2,1,0:T(8,128)(2,1)S(1)}, u32[]{:S(2)}, u32[]{:S(2)}) %collective-permute-start.7) | collective-permute-done | bytes 196640 | tf_op jit(solution)/shard_map/ppermute | solution.py:23
  52.4 0.3 multiply_convert_fusion
  54.6 1.9 %collective-permute-start.8 = (bf16[4,1,48,128]{3,2,1,0:T(8,128)(2,1)S(1)}, bf16[4,1,48,128]{3,2,1,0:T(8,128)(2,1)S(1)}, u32[]{:S(2)}, u32[]{:S(2)}) collective-permute-start(bf16[4,1,48,128]{3,2,1,0:T(8,128)(2,1)S(1)} %get-tuple-element.26), channel_id=1, source_target_pairs={{0,1},{2,3},{4,5},{6,7},{8,9},{10,11},{12,13},{14,15},{16,17},{18,... | collective-permute-start | bytes 147464 | tf_op jit(solution)/shard_map/ppermute | solution.py:23
  56.6 1.3 collective-permute-start.9
  58.4 0.8 copy-done.2
  59.2 0.5 collective-permute-done.9
  62.0 0.3 fusion.122
  62.5 0.6 copy-done.7
  63.3 1.3 collective-permute-start.10
  64.6 3.0 %collective-permute-start.11 = (f32[4,1,12,128]{3,1,2,0:T(1,128)S(1)}, f32[4,1,12,128]{3,1,2,0:T(1,128)S(1)}, u32[]{:S(2)}, u32[]{:S(2)}) collective-permute-start(f32[4,1,12,128]{3,1,2,0:T(1,128)S(1)} %get-tuple-element.40), channel_id=1, source_target_pairs={{0,1},{2,3},{4,5},{6,7},{8,9},{10,11},{12,13},{14,15},{16,17},{18,... | collective-permute-start | bytes 73736 | tf_op jit(solution)/shard_map/ppermute | solution.py:12
  67.7 0.8 collective-permute-done.11
  68.5 0.7 fusion.107
  69.2 84.1 %all-reduce.8.cloned.1.call-done = (f32[3,3,128,128]{3,2,1,0:T(8,128)}, f32[5,128,128]{2,1,0:T(8,128)}) async-done(((f32[3,3,128,128]{3,2,1,0:T(8,128)}, f32[5,128,128]{2,1,0:T(8,128)}), (f32[3,3,128,128]{3,2,1,0:T(8,128)}, f32[5,128,128]{2,1,0:T(8,128)})) %all-reduce.8.cloned.1.call-update) | async-done | bytes 917520 | tf_op jit(solution)/shard_map/psum | solution.py:187
  153.4 2.0 %copy.127 = f32[3,3,128,128]{3,2,1,0:T(8,128)} copy(f32[3,3,128,128]{3,2,1,0:T(8,128)} %get-tuple-element.58) | data formatting | bytes 1179648
  155.3 0.7 copy.128
  (86 shorter events, 11.3 us)
Async XLA Ops:
  7.2 146.2 %all-reduce.8.cloned.1.call-start = ((), (), s32[]{:S(2)}) async-start(), calls=%async_computation | async-start | bytes 1835008 | tf_op jit(solution)/shard_map/psum | solution.py:187
  7.2 6.3 %copy-start.6 = (bf16[4,1,12,128]{3,0,2,1:T(4,128)(2,1)S(1)}, bf16[4,1,12,128]{3,0,2,1:T(4,128)(2,1)}, u32[]{:S(2)}) copy-start(bf16[4,1,12,128]{3,0,2,1:T(4,128)(2,1)} %param.4) | copy-start | bytes 36868
  8.0 3.7 %collective-permute-start = (bf16[4,1,12,128]{3,1,2,0:T(2,128)(2,1)S(1)}, bf16[4,1,12,128]{3,1,2,0:T(2,128)(2,1)S(1)}, u32[]{:S(2)}, u32[]{:S(2)}) collective-permute-start(bf16[4,1,12,128]{3,1,2,0:T(2,128)(2,1)S(1)} %copy.55), channel_id=1, source_target_pairs={{0,1},{2,3},{4,5},{6,7},{8,9},{10,11},{12,13},{14,15},{16,17},{18,... | collective-permute-start | bytes 36872 | tf_op jit(solution)/shard_map/ppermute | solution.py:23
  10.4 3.1 %collective-permute-start.1 = (bf16[4,1,12,128]{3,1,2,0:T(2,128)(2,1)S(1)}, bf16[4,1,12,128]{3,1,2,0:T(2,128)(2,1)S(1)}, u32[]{:S(2)}, u32[]{:S(2)}) collective-permute-start(bf16[4,1,12,128]{3,1,2,0:T(2,128)(2,1)S(1)} %copy.55), channel_id=1, source_target_pairs={{1,0},{3,2},{5,4},{7,6},{9,8},{11,10},{13,12},{15,14},{17,16},{19,... | collective-permute-start | bytes 36872 | tf_op jit(solution)/shard_map/ppermute | solution.py:25
  14.4 3.4 %collective-permute-start.2 = (bf16[4,1,48,128]{3,2,1,0:T(8,128)(2,1)S(1)}, bf16[4,1,48,128]{3,2,1,0:T(8,128)(2,1)S(1)}, u32[]{:S(2)}, u32[]{:S(2)}) collective-permute-start(bf16[4,1,48,128]{3,2,1,0:T(8,128)(2,1)S(1)} %get-tuple-element.34), channel_id=1, source_target_pairs={{0,1},{2,3},{4,5},{6,7},{8,9},{10,11},{12,13},{14,15},{16,17},{18,... | collective-permute-start | bytes 147464 | tf_op jit(solution)/shard_map/ppermute | solution.py:23
  16.5 3.1 %collective-permute-start.3 = (bf16[4,1,48,128]{3,2,1,0:T(8,128)(2,1)S(1)}, bf16[4,1,48,128]{3,2,1,0:T(8,128)(2,1)S(1)}, u32[]{:S(2)}, u32[]{:S(2)}) collective-permute-start(bf16[4,1,48,128]{3,2,1,0:T(8,128)(2,1)S(1)} %get-tuple-element.35), channel_id=1, source_target_pairs={{1,0},{3,2},{5,4},{7,6},{9,8},{11,10},{13,12},{15,14},{17,16},{19,... | collective-permute-start | bytes 147464 | tf_op jit(solution)/shard_map/ppermute | solution.py:25
  19.7 1.0 copy-start
  22.5 5.7 %copy-start.3 = (bf16[5,128,128]{2,1,0:T(8,128)(2,1)S(1)}, bf16[5,128,128]{2,1,0:T(8,128)(2,1)}, u32[]{:S(2)}) copy-start(bf16[5,128,128]{2,1,0:T(8,128)(2,1)} %param.7) | copy-start | bytes 491524
  22.7 8.8 %collective-permute-start.4 = (bf16[4,4,48,128]{3,2,1,0:T(8,128)(2,1)S(1)}, bf16[4,4,48,128]{3,2,1,0:T(8,128)(2,1)S(1)}, u32[]{:S(2)}, u32[]{:S(2)}) collective-permute-start(bf16[4,4,48,128]{3,2,1,0:T(8,128)(2,1)S(1)} %multiply_convert_fusion.3), channel_id=1, source_target_pairs={{0,2},{2,4},{4,6},{6,8},{8,10},{10,12},{12,14},{1,3},{3,5},{5,7},{... | collective-permute-start | bytes 589832 | tf_op jit(solution)/shard_map/ppermute | solution.py:23
  26.9 8.6 %collective-permute-start.5 = (bf16[4,4,48,128]{3,2,1,0:T(8,128)(2,1)S(1)}, bf16[4,4,48,128]{3,2,1,0:T(8,128)(2,1)S(1)}, u32[]{:S(2)}, u32[]{:S(2)}) collective-permute-start(bf16[4,4,48,128]{3,2,1,0:T(8,128)(2,1)S(1)} %multiply_convert_fusion.3), channel_id=1, source_target_pairs={{2,0},{4,2},{6,4},{8,6},{10,8},{12,10},{14,12},{3,1},{5,3},{7,5},{... | collective-permute-start | bytes 589832 | tf_op jit(solution)/shard_map/ppermute | solution.py:25
  36.1 0.9 copy-start.1
  37.9 8.5 %collective-permute-start.6 = (bf16[4,4,48,128]{3,2,1,0:T(8,128)(2,1)S(1)}, bf16[4,4,48,128]{3,2,1,0:T(8,128)(2,1)S(1)}, u32[]{:S(2)}, u32[]{:S(2)}) collective-permute-start(bf16[4,4,48,128]{3,2,1,0:T(8,128)(2,1)S(1)} %get-tuple-element.10), channel_id=1, source_target_pairs={{2,0},{4,2},{6,4},{8,6},{10,8},{12,10},{14,12},{3,1},{5,3},{7,5},{... | collective-permute-start | bytes 589832 | tf_op jit(solution)/shard_map/ppermute | solution.py:25
  39.2 12.4 %collective-permute-start.7 = (bf16[4,4,48,128]{3,2,1,0:T(8,128)(2,1)S(1)}, bf16[4,4,48,128]{3,2,1,0:T(8,128)(2,1)S(1)}, u32[]{:S(2)}, u32[]{:S(2)}) collective-permute-start(bf16[4,4,48,128]{3,2,1,0:T(8,128)(2,1)S(1)} %get-tuple-element.10), channel_id=1, source_target_pairs={{0,2},{2,4},{4,6},{6,8},{8,10},{10,12},{12,14},{1,3},{3,5},{5,7},{... | collective-permute-start | bytes 589832 | tf_op jit(solution)/shard_map/ppermute | solution.py:23
  45.9 5.8 %copy-start.4 = (f32[5,128,128]{2,1,0:T(8,128)}, f32[5,128,128]{2,1,0:T(8,128)S(1)}, u32[]{:S(2)}) copy-start(f32[5,128,128]{2,1,0:T(8,128)S(1)} %fusion.10) | copy-start | bytes 983044
  54.6 4.6 %collective-permute-start.8 = (bf16[4,1,48,128]{3,2,1,0:T(8,128)(2,1)S(1)}, bf16[4,1,48,128]{3,2,1,0:T(8,128)(2,1)S(1)}, u32[]{:S(2)}, u32[]{:S(2)}) collective-permute-start(bf16[4,1,48,128]{3,2,1,0:T(8,128)(2,1)S(1)} %get-tuple-element.26), channel_id=1, source_target_pairs={{0,1},{2,3},{4,5},{6,7},{8,9},{10,11},{12,13},{14,15},{16,17},{18,... | collective-permute-start | bytes 147464 | tf_op jit(solution)/shard_map/ppermute | solution.py:23
  56.6 3.1 %collective-permute-start.9 = (bf16[4,1,48,128]{3,2,1,0:T(8,128)(2,1)S(1)}, bf16[4,1,48,128]{3,2,1,0:T(8,128)(2,1)S(1)}, u32[]{:S(2)}, u32[]{:S(2)}) collective-permute-start(bf16[4,1,48,128]{3,2,1,0:T(8,128)(2,1)S(1)} %get-tuple-element.27), channel_id=1, source_target_pairs={{1,0},{3,2},{5,4},{7,6},{9,8},{11,10},{13,12},{15,14},{17,16},{19,... | collective-permute-start | bytes 147464 | tf_op jit(solution)/shard_map/ppermute | solution.py:25
  58.4 0.8 copy-start.2
  62.4 0.7 copy-start.7
  63.3 4.3 %collective-permute-start.10 = (f32[4,1,12,128]{3,1,2,0:T(1,128)S(1)}, f32[4,1,12,128]{3,1,2,0:T(1,128)S(1)}, u32[]{:S(2)}, u32[]{:S(2)}) collective-permute-start(f32[4,1,12,128]{3,1,2,0:T(1,128)S(1)} %get-tuple-element.41), channel_id=1, source_target_pairs={{1,0},{3,2},{5,4},{7,6},{9,8},{11,10},{13,12},{15,14},{17,16},{19,... | collective-permute-start | bytes 73736 | tf_op jit(solution)/shard_map/ppermute | solution.py:12
  64.6 3.9 %collective-permute-start.11 = (f32[4,1,12,128]{3,1,2,0:T(1,128)S(1)}, f32[4,1,12,128]{3,1,2,0:T(1,128)S(1)}, u32[]{:S(2)}, u32[]{:S(2)}) collective-permute-start(f32[4,1,12,128]{3,1,2,0:T(1,128)S(1)} %get-tuple-element.40), channel_id=1, source_target_pairs={{0,1},{2,3},{4,5},{6,7},{8,9},{10,11},{12,13},{14,15},{16,17},{18,... | collective-permute-start | bytes 73736 | tf_op jit(solution)/shard_map/ppermute | solution.py:12
  153.4 2.0 %copy-start.5 = (f32[5,128,128]{2,1,0:T(8,128)S(1)}, f32[5,128,128]{2,1,0:T(8,128)}, u32[]{:S(2)}) copy-start(f32[5,128,128]{2,1,0:T(8,128)} %get-tuple-element.59) | copy-start | bytes 983044
Sparse Core Ops, SparseCore 0:
  59.3 93.9 all-reduce.7
where the time goes:
time: 163 us
  waiting for transfers between devices  102 us (63%)
  starting transfers between devices  26.5 us (16%)
  between operations  14.7 us (9%)
  matrix products  9.25 us (6%)
  local copies, waits for them, and re-layouts  7.29 us (4%)
  other arithmetic  3.34 us (2%)
    psum x1, waiting for transfers between devices, local(): grad_spatial = lax.psum(spatial_local, ('space', 'tm'))  84.1 us
    ppermute x5, starting transfers between devices, extended(): lax.ppermute(tail, axis, [(i, (i + 1) % count) for i in range(ends)])  15.7 us
    ppermute x5, waiting for transfers between devices, extended(): lax.ppermute(head, axis, [((i + 1) % count, i) for i in range(ends)])  8.69 us
    ppermute x5, waiting for transfers between devices, extended(): lax.ppermute(tail, axis, [(i, (i + 1) % count) for i in range(ends)])  8.19 us
    ppermute x5, starting transfers between devices, extended(): lax.ppermute(head, axis, [((i + 1) % count, i) for i in range(ends)])  6.45 us
    unnamed x19, local copies, waits for them, and re-layouts  6.45 us
    ppermute x2, starting transfers between devices, shifted(): return lax.ppermute(value, axis, pairs)  4.32 us
    dot_general x18, matrix products, conv_three(): jnp.dot(frame_window, kernel, preferred_element_type=jnp.float32)  3.61 us
  transfers between devices with their start and end apart: 13, of which 9 were waited for; matrix products, arithmetic and copies ran while one was open for 4% of the time, Pallas kernels for 0%

commit v1 on v0

--- a/solution.py
+++ b/solution.py
@@ -184,7 +184,7 @@
     delta_pad = jnp.pad(delta_rows, ((0, 0), (0, 0), (1, 1), (0, 0)))
     grad_image = upstream + conv_three(delta_pad, w_spatial, row_count, col_count, 2)
     grad_base = shrink_base(grad_image, row_rank, row_devices, base_latent.shape)
-    grad_spatial = lax.psum(spatial_local, ("space", "tm"))
+    grad_spatial = jnp.sum(lax.all_gather(spatial_local, ("space", "tm")), axis=0)
     return (result, grad_base, grad_spatial, grad_temporal)
 
 

time: 163 us -> 242 us (1.48)
  waiting for transfers between devices: 102 us -> 173 us
  other arithmetic: 3.34 us -> 9.22 us
  matrix products: 9.25 us -> 13 us
    all_gather x0 -> x1, waiting for transfers between devices: none -> 68.1 us  [local(): lax.all_gather(spatial_local, ('space', 'tm'))]
    reduce_sum x0 -> x1, other arithmetic: none -> 5.18 us  [local(): jnp.sum(lax.all_gather(spatial_local, ('space', 'tm')), axis=0)]
    dot_general x18, matrix products: 3.61 us -> 7.41 us  [conv_three(): jnp.dot(frame_window, kernel, preferred_element_type=jnp.float32)]
    unnamed x19 -> x14, local copies, waits for them, and re-layouts: 6.45 us -> 4.03 us
  transfers between devices with their start and end apart: 13 -> 14, of which waited for: 9 -> 9; matrix products, arithmetic and copies ran while one was open for 4% -> 4% of each run, Pallas kernels for 0% -> 0%
where the time goes in v1:
time: 242 us; the launch traced here: 241 us
  waiting for transfers between devices  173 us (71%)
  starting transfers between devices  26.5 us (11%)
  between operations  14.7 us (6%)
  matrix products  13 us (5%)
  other arithmetic  9.22 us (4%)
  local copies, waits for them, and re-layouts  4.88 us (2%)
    psum x1, waiting for transfers between devices, local(): grad_temporal = lax.psum(temporal_local, ('space', 'tm'))  85.4 us
    all_gather x1, waiting for transfers between devices, local(): lax.all_gather(spatial_local, ('space', 'tm'))  68.1 us
    ppermute x5, starting transfers between devices, extended(): lax.ppermute(tail, axis, [(i, (i + 1) % count) for i in range(ends)])  15.7 us
    ppermute x5, waiting for transfers between devices, extended(): lax.ppermute(head, axis, [((i + 1) % count, i) for i in range(ends)])  11.1 us
    ppermute x5, waiting for transfers between devices, extended(): lax.ppermute(tail, axis, [(i, (i + 1) % count) for i in range(ends)])  8.23 us
    dot_general x18, matrix products, conv_three(): jnp.dot(frame_window, kernel, preferred_element_type=jnp.float32)  7.41 us
    ppermute x5, starting transfers between devices, extended(): lax.ppermute(head, axis, [((i + 1) % count, i) for i in range(ends)])  6.45 us
    reduce_sum x1, other arithmetic, local(): jnp.sum(lax.all_gather(spatial_local, ('space', 'tm')), axis=0)  5.18 us
  transfers between devices with their start and end apart: 14, of which 9 were waited for; matrix products, arithmetic and copies ran while one was open for 4% of the time, Pallas kernels for 0%

profile of v1, /device:TPU:0, one launch (start us, length us, event | category | flops | bytes accessed | tf_op | source)
XLA Modules:
  0.0 241.2 jit_solution(15015682370104539081)
XLA Ops:
  7.2 0.8 copy.75
  8.0 2.4 collective-permute-start
  10.4 1.3 collective-permute-start.1
  11.7 1.8 collective-permute-done.1
  13.5 0.8 add_bitcast_fusion.7
  15.1 2.1 collective-permute-start.2
  17.2 1.3 collective-permute-start.3
  18.5 1.8 collective-permute-done.3
  20.6 0.9 fusion.75
  21.6 0.9 fusion.57
  22.6 1.0 convolution_add_fusion.17
  23.5 0.9 convolution_add_fusion.16
  24.5 1.0 convolution_add_fusion.15
  26.4 4.2 %collective-permute-start.4 = (bf16[4,4,48,128]{3,2,1,0:T(8,128)(2,1)S(1)}, bf16[4,4,48,128]{3,2,1,0:T(8,128)(2,1)S(1)}, u32[]{:S(2)}, u32[]{:S(2)}) collective-permute-start(bf16[4,4,48,128]{3,2,1,0:T(8,128)(2,1)S(1)} %multiply_convert_fusion.3), channel_id=1, source_target_pairs={{0,2},{2,4},{4,6},{6,8},{8,10},{10,12},{12,14},{1,3},{3,5},{5,7},{... | collective-permute-start | bytes 589832 | tf_op jit(solution)/shard_map/ppermute | solution.py:23
  30.6 1.3 collective-permute-start.5
  32.1 3.0 %collective-permute-done.4 = bf16[4,4,48,128]{3,2,1,0:T(8,128)(2,1)S(1)} collective-permute-done((bf16[4,4,48,128]{3,2,1,0:T(8,128)(2,1)S(1)}, bf16[4,4,48,128]{3,2,1,0:T(8,128)(2,1)S(1)}, u32[]{:S(2)}, u32[]{:S(2)}) %collective-permute-start.4) | collective-permute-done | bytes 196640 | tf_op jit(solution)/shard_map/ppermute | solution.py:23
  35.1 4.0 %collective-permute-done.5 = bf16[4,4,48,128]{3,2,1,0:T(8,128)(2,1)S(1)} collective-permute-done((bf16[4,4,48,128]{3,2,1,0:T(8,128)(2,1)S(1)}, bf16[4,4,48,128]{3,2,1,0:T(8,128)(2,1)S(1)}, u32[]{:S(2)}, u32[]{:S(2)}) %collective-permute-start.5) | collective-permute-done | bytes 196640 | tf_op jit(solution)/shard_map/ppermute | solution.py:25
  40.0 0.9 fusion.21
  40.9 1.3 collective-permute-start.6
  42.2 5.1 %collective-permute-start.7 = (bf16[4,4,48,128]{3,2,1,0:T(8,128)(2,1)S(1)}, bf16[4,4,48,128]{3,2,1,0:T(8,128)(2,1)S(1)}, u32[]{:S(2)}, u32[]{:S(2)}) collective-permute-start(bf16[4,4,48,128]{3,2,1,0:T(8,128)(2,1)S(1)} %get-tuple-element.8), channel_id=1, source_target_pairs={{0,2},{2,4},{4,6},{6,8},{8,10},{10,12},{12,14},{1,3},{3,5},{5,7},{... | collective-permute-start | bytes 589832 | tf_op jit(solution)/shard_map/ppermute | solution.py:23
  47.5 1.9 collective-permute-done.6
  49.4 5.2 %collective-permute-done.7 = bf16[4,4,48,128]{3,2,1,0:T(8,128)(2,1)S(1)} collective-permute-done((bf16[4,4,48,128]{3,2,1,0:T(8,128)(2,1)S(1)}, bf16[4,4,48,128]{3,2,1,0:T(8,128)(2,1)S(1)}, u32[]{:S(2)}, u32[]{:S(2)}) %collective-permute-start.7) | collective-permute-done | bytes 196640 | tf_op jit(solution)/shard_map/ppermute | solution.py:23
  58.1 0.8 copy-done.2
  59.8 1.9 collective-permute-start.8
  61.7 1.3 collective-permute-start.9
  63.3 1.6 collective-permute-done.9
  67.9 1.3 collective-permute-start.10
  69.2 3.0 %collective-permute-start.11 = (f32[4,1,12,128]{3,1,2,0:T(1,128)S(1)}, f32[4,1,12,128]{3,1,2,0:T(1,128)S(1)}, u32[]{:S(2)}, u32[]{:S(2)}) collective-permute-start(f32[4,1,12,128]{3,1,2,0:T(1,128)S(1)} %get-tuple-element.38), channel_id=1, source_target_pairs={{0,1},{2,3},{4,5},{6,7},{8,9},{10,11},{12,13},{14,15},{16,17},{18,... | collective-permute-start | bytes 73736 | tf_op jit(solution)/shard_map/ppermute | solution.py:12
  74.0 68.1 %all-gather.2.cloned.1.call-done = f32[16,3,3,128,128]{4,3,2,1,0:T(8,128)} async-done(((f32[1,3,3,128,128]{4,3,2,1,0:T(8,128)}), f32[16,3,3,128,128]{4,3,2,1,0:T(8,128)}) %all-gather.2.cloned.1.call-update) | async-done | bytes 9437200 | tf_op jit(solution)/shard_map/all_gather | solution.py:187
  142.1 5.2 %reduce_sum.9 = f32[3,3,128,128]{3,2,1,0:T(8,128)} reduce(f32[16,3,3,128,128]{4,3,2,1,0:T(8,128)} %all-gather.2.cloned.1.call-done, f32[]{:T(128)} %constant.9.clone.1), dimensions={0}, to_apply=%region_0.1 | reduce | flops 2211840 | bytes 10027012 | tf_op jit(solution)/shard_map/reduce_sum | solution.py:187
  147.2 85.4 %all-reduce.7.cloned.1.call-done = f32[5,128,128]{2,1,0:T(8,128)} async-done(((f32[5,128,128]{2,1,0:T(8,128)}), f32[5,128,128]{2,1,0:T(8,128)}) %all-reduce.7.cloned.1.call-update) | async-done | bytes 327696 | tf_op jit(solution)/shard_map/psum | solution.py:178
  232.6 1.7 copy.146
  (85 shorter events, 12.3 us)
Async XLA Ops:
  7.2 18.3 %copy-start = (bf16[3,3,128,128]{3,2,1,0:T(8,128)(2,1)S(1)}, bf16[3,3,128,128]{3,2,1,0:T(8,128)(2,1)}, u32[]{:S(2)}) copy-start(bf16[3,3,128,128]{3,2,1,0:T(8,128)(2,1)} %param.6) | copy-start | bytes 884740
  7.2 24.7 %copy-start.3 = (bf16[5,128,128]{2,1,0:T(8,128)(2,1)S(1)}, bf16[5,128,128]{2,1,0:T(8,128)(2,1)}, u32[]{:S(2)}) copy-start(bf16[5,128,128]{2,1,0:T(8,128)(2,1)} %param.7) | copy-start | bytes 491524
  7.2 134.9 %all-gather.2.cloned.1.call-start = ((), (), s32[]{:S(2)}) async-start(), calls=%async_computation | async-start | bytes 10027008 | tf_op jit(solution)/shard_map/all_gather | solution.py:187
  8.0 3.7 %collective-permute-start = (bf16[4,1,12,128]{3,1,2,0:T(2,128)(2,1)S(1)}, bf16[4,1,12,128]{3,1,2,0:T(2,128)(2,1)S(1)}, u32[]{:S(2)}, u32[]{:S(2)}) collective-permute-start(bf16[4,1,12,128]{3,1,2,0:T(2,128)(2,1)S(1)} %copy.75), channel_id=1, source_target_pairs={{0,1},{2,3},{4,5},{6,7},{8,9},{10,11},{12,13},{14,15},{16,17},{18,... | collective-permute-start | bytes 36872 | tf_op jit(solution)/shard_map/ppermute | solution.py:23
  10.4 3.1 %collective-permute-start.1 = (bf16[4,1,12,128]{3,1,2,0:T(2,128)(2,1)S(1)}, bf16[4,1,12,128]{3,1,2,0:T(2,128)(2,1)S(1)}, u32[]{:S(2)}, u32[]{:S(2)}) collective-permute-start(bf16[4,1,12,128]{3,1,2,0:T(2,128)(2,1)S(1)} %copy.75), channel_id=1, source_target_pairs={{1,0},{3,2},{5,4},{7,6},{9,8},{11,10},{13,12},{15,14},{17,16},{19,... | collective-permute-start | bytes 36872 | tf_op jit(solution)/shard_map/ppermute | solution.py:25
  15.1 3.4 %collective-permute-start.2 = (bf16[4,1,48,128]{3,2,1,0:T(8,128)(2,1)S(1)}, bf16[4,1,48,128]{3,2,1,0:T(8,128)(2,1)S(1)}, u32[]{:S(2)}, u32[]{:S(2)}) collective-permute-start(bf16[4,1,48,128]{3,2,1,0:T(8,128)(2,1)S(1)} %get-tuple-element.32), channel_id=1, source_target_pairs={{0,1},{2,3},{4,5},{6,7},{8,9},{10,11},{12,13},{14,15},{16,17},{18,... | collective-permute-start | bytes 147464 | tf_op jit(solution)/shard_map/ppermute | solution.py:23
  17.2 3.1 %collective-permute-start.3 = (bf16[4,1,48,128]{3,2,1,0:T(8,128)(2,1)S(1)}, bf16[4,1,48,128]{3,2,1,0:T(8,128)(2,1)S(1)}, u32[]{:S(2)}, u32[]{:S(2)}) collective-permute-start(bf16[4,1,48,128]{3,2,1,0:T(8,128)(2,1)S(1)} %get-tuple-element.33), channel_id=1, source_target_pairs={{1,0},{3,2},{5,4},{7,6},{9,8},{11,10},{13,12},{15,14},{17,16},{19,... | collective-permute-start | bytes 147464 | tf_op jit(solution)/shard_map/ppermute | solution.py:25
  20.4 19.6 %copy-start.1 = (bf16[4,4,48,128]{3,2,1,0:T(8,128)(2,1)S(1)}, bf16[4,4,48,128]{3,2,1,0:T(8,128)(2,1)}, u32[]{:S(2)}) copy-start(bf16[4,4,48,128]{3,2,1,0:T(8,128)(2,1)} %param.5) | copy-start | bytes 589828
  26.4 8.8 %collective-permute-start.4 = (bf16[4,4,48,128]{3,2,1,0:T(8,128)(2,1)S(1)}, bf16[4,4,48,128]{3,2,1,0:T(8,128)(2,1)S(1)}, u32[]{:S(2)}, u32[]{:S(2)}) collective-permute-start(bf16[4,4,48,128]{3,2,1,0:T(8,128)(2,1)S(1)} %multiply_convert_fusion.3), channel_id=1, source_target_pairs={{0,2},{2,4},{4,6},{6,8},{8,10},{10,12},{12,14},{1,3},{3,5},{5,7},{... | collective-permute-start | bytes 589832 | tf_op jit(solution)/shard_map/ppermute | solution.py:23
  30.6 8.6 %collective-permute-start.5 = (bf16[4,4,48,128]{3,2,1,0:T(8,128)(2,1)S(1)}, bf16[4,4,48,128]{3,2,1,0:T(8,128)(2,1)S(1)}, u32[]{:S(2)}, u32[]{:S(2)}) collective-permute-start(bf16[4,4,48,128]{3,2,1,0:T(8,128)(2,1)S(1)} %multiply_convert_fusion.3), channel_id=1, source_target_pairs={{2,0},{4,2},{6,4},{8,6},{10,8},{12,10},{14,12},{3,1},{5,3},{7,5},{... | collective-permute-start | bytes 589832 | tf_op jit(solution)/shard_map/ppermute | solution.py:25
  40.9 8.5 %collective-permute-start.6 = (bf16[4,4,48,128]{3,2,1,0:T(8,128)(2,1)S(1)}, bf16[4,4,48,128]{3,2,1,0:T(8,128)(2,1)S(1)}, u32[]{:S(2)}, u32[]{:S(2)}) collective-permute-start(bf16[4,4,48,128]{3,2,1,0:T(8,128)(2,1)S(1)} %get-tuple-element.8), channel_id=1, source_target_pairs={{2,0},{4,2},{6,4},{8,6},{10,8},{12,10},{14,12},{3,1},{5,3},{7,5},{... | collective-permute-start | bytes 589832 | tf_op jit(solution)/shard_map/ppermute | solution.py:25
  42.2 12.4 %collective-permute-start.7 = (bf16[4,4,48,128]{3,2,1,0:T(8,128)(2,1)S(1)}, bf16[4,4,48,128]{3,2,1,0:T(8,128)(2,1)S(1)}, u32[]{:S(2)}, u32[]{:S(2)}) collective-permute-start(bf16[4,4,48,128]{3,2,1,0:T(8,128)(2,1)S(1)} %get-tuple-element.8), channel_id=1, source_target_pairs={{0,2},{2,4},{4,6},{6,8},{8,10},{10,12},{12,14},{1,3},{3,5},{5,7},{... | collective-permute-start | bytes 589832 | tf_op jit(solution)/shard_map/ppermute | solution.py:23
  58.1 0.8 copy-start.2
  58.1 9.5 %copy-start.5 = (pred[12]{0:T(512)(128)(4,1)S(1)}, pred[12]{0:T(512)(128)(4,1)}, u32[]{:S(2)}) copy-start(pred[12]{0:T(512)(128)(4,1)} %constant.10.clone.1) | copy-start | bytes 40
  58.9 173.7 %all-reduce.7.cloned.1.call-start = ((), (), s32[]{:S(2)}) async-start(), calls=%async_computation.1 | async-start | bytes 655360 | tf_op jit(solution)/shard_map/psum | solution.py:178
  59.8 3.5 %collective-permute-start.8 = (bf16[4,1,48,128]{3,2,1,0:T(8,128)(2,1)S(1)}, bf16[4,1,48,128]{3,2,1,0:T(8,128)(2,1)S(1)}, u32[]{:S(2)}, u32[]{:S(2)}) collective-permute-start(bf16[4,1,48,128]{3,2,1,0:T(8,128)(2,1)S(1)} %get-tuple-element.24), channel_id=1, source_target_pairs={{0,1},{2,3},{4,5},{6,7},{8,9},{10,11},{12,13},{14,15},{16,17},{18,... | collective-permute-start | bytes 147464 | tf_op jit(solution)/shard_map/ppermute | solution.py:23
  61.7 3.1 %collective-permute-start.9 = (bf16[4,1,48,128]{3,2,1,0:T(8,128)(2,1)S(1)}, bf16[4,1,48,128]{3,2,1,0:T(8,128)(2,1)S(1)}, u32[]{:S(2)}, u32[]{:S(2)}) collective-permute-start(bf16[4,1,48,128]{3,2,1,0:T(8,128)(2,1)S(1)} %get-tuple-element.25), channel_id=1, source_target_pairs={{1,0},{3,2},{5,4},{7,6},{9,8},{11,10},{13,12},{15,14},{17,16},{19,... | collective-permute-start | bytes 147464 | tf_op jit(solution)/shard_map/ppermute | solution.py:25
  67.9 5.3 %collective-permute-start.10 = (f32[4,1,12,128]{3,1,2,0:T(1,128)S(1)}, f32[4,1,12,128]{3,1,2,0:T(1,128)S(1)}, u32[]{:S(2)}, u32[]{:S(2)}) collective-permute-start(f32[4,1,12,128]{3,1,2,0:T(1,128)S(1)} %get-tuple-element.39), channel_id=1, source_target_pairs={{1,0},{3,2},{5,4},{7,6},{9,8},{11,10},{13,12},{15,14},{17,16},{19,... | collective-permute-start | bytes 73736 | tf_op jit(solution)/shard_map/ppermute | solution.py:12
  69.2 4.1 %collective-permute-start.11 = (f32[4,1,12,128]{3,1,2,0:T(1,128)S(1)}, f32[4,1,12,128]{3,1,2,0:T(1,128)S(1)}, u32[]{:S(2)}, u32[]{:S(2)}) collective-permute-start(f32[4,1,12,128]{3,1,2,0:T(1,128)S(1)} %get-tuple-element.38), channel_id=1, source_target_pairs={{0,1},{2,3},{4,5},{6,7},{8,9},{10,11},{12,13},{14,15},{16,17},{18,... | collective-permute-start | bytes 73736 | tf_op jit(solution)/shard_map/ppermute | solution.py:12
  72.4 0.7 copy-start.4
Sparse Core Ops, SparseCore 0:
  59.1 82.9 all-gather.1
  146.0 86.5 all-reduce.6
